TPU v7x, 32 devices: a whole 2x2x4 slice. The times are simulated.
32 devices in a mesh: grp: 2 (over y), gx: 16 (over z, x, core).
Axes of the slice: x: 2, y: 2, z: 4, core: 2. Of those that a mesh axis runs over, the one named last changes fastest.
Arguments:
- mesh_feature_array: bfloat16 [128, 32, 32, 512], P(('grp', 'gx')), parts along dimension 0, may hold values from -6 to 6
- stencil_coefficients: float32 [27, 512], replicated, may hold values from -1.25 to 1.25
- partition_affinity_matrix: bfloat16 [512, 512], replicated, may hold values from -16 to 16
- softness_mapping_matrix: float32 [512], replicated, may hold values from -0.25 to 0.25
- content_mapping_matrix: bfloat16 [512, 512], replicated, may hold values from -0.25 to 0.25
- layernorm_multiplier: float32 [512], replicated, may hold values from 0.1 to 1.9
- widening_matrix: bfloat16 [512, 1024], replicated, may hold values from -0.25 to 0.25
- narrowing_matrix: bfloat16 [1024, 512], replicated, may hold values from -0.1875 to 0.1875
- final_mapping_matrix: bfloat16 [512, 512], replicated, may hold values from -0.25 to 0.25
Outputs:
- updated: bfloat16 [128, 32, 32, 512], P(('grp', 'gx')), parts along dimension 0
- slice_out: bfloat16 [1024, 512], P(('grp', 'gx')), parts along dimension 0
There are 2 independent parts, one for each index of `grp`. A program takes and returns all parts, laid end to end along the dimension named above; an argument that names none is the same for every part. Nothing has to cross between parts.
All inputs are finite; a program needn't handle non-finite values.
Results may differ from a plain program's by a relative error of at most 0.0056.
Values may be sent and summed in bfloat16 or wider, within the bound.
A program may use at most 128 MiB of HBM per device.

v0:
```python
import jax
import jax.numpy as jnp
from jax import lax
from jax.sharding import PartitionSpec as P

epsilon = 1e-05


def padded_2(value, sides, width):
    for axis, dim in sides:
        size, length = (lax.axis_size(axis), value.shape[dim])
        up = [(i, (i + 1) % size) for i in range(size - 1)]
        down = [(j, i) for i, j in up]
        last = lax.slice_in_dim(value, length - width, length, axis=dim)
        initial = lax.slice_in_dim(value, 0, width, axis=dim)
        before = lax.ppermute(last, axis, up)
        after = lax.ppermute(initial, axis, down)
        value = jnp.concatenate([before, value, after], axis=dim)
    return value


def owner_mlp(tokens, layernorm_multiplier, widening_matrix, narrowing_matrix):
    center = jnp.mean(tokens, axis=-1, keepdims=True)
    spread = jnp.mean((tokens - center) ** 2, axis=-1, keepdims=True)
    normed = ((tokens - center) * (1.0 / jnp.sqrt(spread + epsilon)) * layernorm_multiplier).astype(
        jnp.bfloat16
    )
    inner = jax.nn.gelu(
        jnp.dot(normed, widening_matrix, preferred_element_type=jnp.float32)
    ).astype(jnp.bfloat16)
    return (tokens + jnp.dot(inner, narrowing_matrix, preferred_element_type=jnp.float32)).astype(
        jnp.bfloat16
    )


def per_device(
    mesh_feature_array,
    stencil_coefficients,
    partition_affinity_matrix,
    softness_mapping_matrix,
    content_mapping_matrix,
    layernorm_multiplier,
    widening_matrix,
    narrowing_matrix,
    final_mapping_matrix,
):
    planes, rows_y, rows_z, channels = mesh_feature_array.shape
    padded = padded_2(mesh_feature_array, (("gx", 0),), 1)
    padded = jnp.pad(padded, ((0, 0), (1, 1), (1, 1), (0, 0)))
    total = jnp.zeros((planes, rows_y, rows_z, channels), jnp.float32)
    for offset_a in range(3):
        for offset_b in range(3):
            for offset_c in range(3):
                window = padded[
                    offset_a : offset_a + planes,
                    offset_b : offset_b + rows_y,
                    offset_c : offset_c + rows_z,
                ]
                total = (
                    total
                    + window.astype(jnp.float32)
                    * stencil_coefficients[9 * offset_a + 3 * offset_b + offset_c]
                )
    intermediate_response = jax.nn.gelu(total).astype(jnp.bfloat16).reshape(-1, channels)
    local_softness_factor = 0.25 + jax.nn.softplus(
        jnp.dot(
            intermediate_response,
            softness_mapping_matrix.astype(jnp.bfloat16),
            preferred_element_type=jnp.float32,
        )
    )
    partition_affinity_raw = (
        jnp.dot(
            intermediate_response, partition_affinity_matrix, preferred_element_type=jnp.float32
        )
        / local_softness_factor[:, None]
    )
    slice_probs = jax.nn.softmax(partition_affinity_raw, axis=-1).astype(jnp.bfloat16)
    values = jnp.dot(
        intermediate_response, content_mapping_matrix, preferred_element_type=jnp.float32
    ).astype(jnp.bfloat16)
    weighted_token_share = lax.dot_general(
        slice_probs, values, (((0,), (0,)), ((), ())), preferred_element_type=jnp.float32
    )
    mass_part = jnp.sum(slice_probs.astype(jnp.float32), axis=0)
    weighted_tokens, mass = (
        lax.psum_scatter(weighted_token_share, "gx", scatter_dimension=0, tiled=True),
        lax.psum_scatter(mass_part, "gx", scatter_dimension=0, tiled=True),
    )
    own_out = owner_mlp(
        weighted_tokens / (mass[:, None] + epsilon),
        layernorm_multiplier,
        widening_matrix,
        narrowing_matrix,
    )
    slice_out = lax.all_gather(own_out, "gx", axis=0, tiled=True)
    desliced = jnp.dot(slice_probs, slice_out, preferred_element_type=jnp.float32).astype(
        jnp.bfloat16
    )
    flat = mesh_feature_array.reshape(-1, channels).astype(jnp.float32)
    updated = (
        flat + jnp.dot(desliced, final_mapping_matrix, preferred_element_type=jnp.float32)
    ).astype(jnp.bfloat16)
    return (updated.reshape(planes, rows_y, rows_z, channels), own_out)


def solution(mesh):
    return jax.shard_map(
        per_device,
        mesh=mesh,
        in_specs=(P(("grp", "gx"), None, None, None), P(), P(), P(), P(), P(), P(), P(), P()),
        out_specs=(P(("grp", "gx"), None, None, None), P(("grp", "gx"), None)),
        check_vma=False,
    )
```

profile of v0, /device:TPU:0, one launch (start us, length us, event | category | flops | bytes accessed | tf_op | source)
XLA Modules:
  0.0 192.9 jit_solution(4667031917017449052)
XLA Ops:
  7.2 0.0 copy-start
  7.2 0.0 reduce-scatter.2.cloned.1.call-start
  7.2 1.8 fusion.44
  9.0 0.0 copy-start.1
  9.0 2.7 %collective-permute-start = (bf16[1,32,32,512]{3,2,1,0:T(8,128)(2,1)S(1)}, bf16[1,32,32,512]{3,2,1,0:T(8,128)(2,1)S(1)}, u32[]{:S(2)}, u32[]{:S(2)}) collective-permute-start(bf16[1,32,32,512]{3,2,1,0:T(8,128)(2,1)S(1)} %get-tuple-element.4), channel_id=1, source_target_pairs={{0,1},{1,2},{2,3},{3,4},{4,5},{5,6},{6,7},{7,8},{8,9},{9,10},{10,1... | collective-permute-start | bytes 3145736 | tf_op jit(solution)/shard_map/ppermute | solution.py:16
  11.7 1.3 collective-permute-start.1
  13.0 0.7 convert_element_type.149
  13.7 1.0 fusion.46
  14.7 1.3 fusion.45
  15.9 0.0 collective-permute-done
  16.0 2.4 %collective-permute-done.1 = bf16[1,32,32,512]{3,2,1,0:T(8,128)(2,1)S(1)} collective-permute-done((bf16[1,32,32,512]{3,2,1,0:T(8,128)(2,1)S(1)}, bf16[1,32,32,512]{3,2,1,0:T(8,128)(2,1)S(1)}, u32[]{:S(2)}, u32[]{:S(2)}) %collective-permute-start.1) | collective-permute-done | bytes 1048608 | tf_op jit(solution)/shard_map/ppermute | solution.py:17
  18.3 5.8 %select_maximum_fusion = bf16[6,34,34,512]{3,2,1,0:T(8,128)(2,1)S(1)} fusion(bf16[1,32,32,512]{3,2,1,0:T(8,128)(2,1)S(1)} %collective-permute-done.1, bf16[4,32,32,512]{3,2,1,0:T(8,128)(2,1)} %param.9, bf16[1,32,32,512]{3,2,1,0:T(8,128)(2,1)S(1)} %collective-permute-done), kind=kLoop, calls=%fused_computation.21 | loop fusion | flops 67473408 | bytes 13393920 | tf_op jit(solution)/shard_map/concatenate | solution.py:18
  24.1 0.0 copy-done.1
  24.1 0.0 copy-start.6
  24.1 33.8 %fusion.10 = bf16[4,32,32,512]{3,2,1,0:T(8,128)(2,1)S(1)} fusion(bf16[6,34,34,512]{3,2,1,0:T(8,128)(2,1)S(1)} %select_maximum_fusion, bf16[1,32,32,512]{3,2,1,0:T(8,128)(2,1)S(1)} %collective-permute-done.1, bf16[4,32,32,512]{3,2,1,0:T(8,128)(2,1)S(1)} %copy-done.1, bf16[1,32,32,512]{3,2,1,0:T(8,128)(2,1)S(1)} %collective-permute-done, f32[512]{0:T(512)S(1)} %bitcast.57, ...), kind=kLoop, calls=%fused_computation.15 | loop fusion | flops 190840832 | bytes 111204352 | tf_op jit(solution)/shard_map/convert_element_type | solution.py:64
  57.9 0.0 copy-start.2
  57.9 1.2 fusion.48
  59.1 0.0 copy-done.6
  59.1 2.5 %fusion.47 = (f32[4096]{0:T(1024)S(1)}, f32[4096,512]{0,1:T(8,128)S(1)}) fusion(f32[4096]{0:T(1024)S(1)} %fusion.38, bf16[4096,512]{1,0:T(8,128)(2,1)S(1)} %bitcast.48, bf16[512,512]{1,0:T(8,128)(2,1)S(1)} %copy-done.6), kind=kOutput, calls=%fused_computation.68 | convolution fusion | flops 2151673856 | bytes 13139968 | tf_op jit(solution)/shard_map/dot_general | solution.py:73
  61.7 0.0 copy-done.2
  61.7 1.3 fusion.15
  63.0 0.0 copy-start.7
  63.0 3.0 %convert_reduce_fusion = (f32[512]{0:T(512)S(1)}, bf16[4096,512]{0,1:T(8,128)(2,1)}) fusion(f32[4096]{0:T(1024)S(1)} %fusion.15, f32[4096,512]{0,1:T(8,128)S(1)} %get-tuple-element.34, f32[4096]{0:T(1024)S(1)} %get-tuple-element.33), kind=kLoop, calls=%fused_computation.18 | loop fusion | flops 10485248 | bytes 12617728 | tf_op jit(solution)/shard_map/reduce_sum | solution.py:85
  66.0 0.0 copy-done.7
  66.0 0.0 copy-start.9
  66.0 0.0 copy-start.3
  66.0 0.0 copy-start.5
  66.0 0.0 copy-start.8
  66.0 9.0 %fusion.17 = f32[512,512]{1,0:T(8,128)} fusion(bf16[4096,512]{0,1:T(8,128)(2,1)} %get-tuple-element.3, bf16[4096,512]{1,0:T(8,128)(2,1)} %bitcast.49, bf16[512,512]{1,0:T(8,128)(2,1)S(1)} %copy-done.7), kind=kOutput, calls=%fused_computation.34 | convolution fusion | flops 4297064448 | bytes 9961472 | tf_op jit(solution)/shard_map/dot_general | solution.py:82
  75.1 0.0 reduce-scatter.2.cloned.1.call-update
  75.1 0.0 copy-done.9
  75.1 0.6 dynamic-slice
  76.3 49.8 %all-reduce.1 = f32[512]{0:T(512)S(1)} all-reduce(f32[512]{0:T(512)S(1)} %get-tuple-element.2), channel_id=3, replica_groups=mesh['grp'=2,'gx'=16] {'gx'}, use_global_device_ids=true, to_apply=%region_4.5.clone | all-reduce | flops 512 | bytes 4096
  126.1 0.1 dynamic-slice_add_fusion
  126.2 27.1 %reduce-scatter.2.cloned.1.call-done = f32[32,512]{1,0:T(8,128)} async-done(((f32[512,512]{1,0:T(8,128)}), f32[32,512]{1,0:T(8,128)}) %reduce-scatter.2.cloned.1.call-update) | async-done | bytes 65552 | tf_op jit(solution)/shard_map/reduce_scatter | solution.py:87
  153.3 1.0 fusion.43
  154.3 1.0 multiply_reduce_fusion
  155.3 0.0 copy-done
  155.4 0.0 copy-done.3
  155.4 0.0 copy-done.5
  155.4 1.5 fusion.16
  156.8 0.0 copy-start.4
  156.8 20.8 %all_gather.3 = bf16[512,512]{1,0:T(8,128)(2,1)S(1)} all-gather(bf16[32,512]{1,0:T(8,128)(2,1)S(1)} %fusion.16), channel_id=1, replica_groups=mesh['grp'=2,'gx'=16] {'gx'}, dimensions={0}, use_global_device_ids=true | all-gather | bytes 557056 | tf_op jit(solution)/shard_map/all_gather | solution.py:96
  177.7 0.0 copy-done.8
  177.7 8.3 %fusion.11 = bf16[4096,512]{1,0:T(8,128)(2,1)} fusion(bf16[512,512]{1,0:T(8,128)(2,1)S(1)} %copy-done.8, bf16[4,32,32,512]{3,2,1,0:T(8,128)(2,1)} %param.9, bf16[4096,512]{0,1:T(8,128)(2,1)} %get-tuple-element.3, bf16[512,512]{1,0:T(8,128)(2,1)S(1)} %all_gather.3), kind=kOutput, calls=%fused_computation.17 | convolution fusion | flops 4303355904 | bytes 13631488 | tf_op jit(solution)/shard_map/dot_general | solution.py:102
  186.0 0.0 copy-done.4
  (4 shorter events, 0.1 us)
Async XLA Ops:
  7.2 148.2 %copy-start = (bf16[1024,512]{1,0:T(8,128)(2,1)S(1)}, bf16[1024,512]{1,0:T(8,128)(2,1)}, u32[]{:S(2)}) copy-start(bf16[1024,512]{1,0:T(8,128)(2,1)} %param.16) | copy-start | bytes 3145732
  7.2 146.1 %reduce-scatter.2.cloned.1.call-start = ((), (), s32[]{:S(2)}) async-start(), calls=%async_computation.1 | async-start | bytes 1114112 | tf_op jit(solution)/shard_map/reduce_scatter | solution.py:87
  9.0 15.1 %copy-start.1 = (bf16[4,32,32,512]{3,2,1,0:T(8,128)(2,1)S(1)}, bf16[4,32,32,512]{3,2,1,0:T(8,128)(2,1)}, u32[]{:S(2)}) copy-start(bf16[4,32,32,512]{3,2,1,0:T(8,128)(2,1)} %param.9) | copy-start | bytes 12582916
  9.0 7.0 %collective-permute-start = (bf16[1,32,32,512]{3,2,1,0:T(8,128)(2,1)S(1)}, bf16[1,32,32,512]{3,2,1,0:T(8,128)(2,1)S(1)}, u32[]{:S(2)}, u32[]{:S(2)}) collective-permute-start(bf16[1,32,32,512]{3,2,1,0:T(8,128)(2,1)S(1)} %get-tuple-element.4), channel_id=1, source_target_pairs={{0,1},{1,2},{2,3},{3,4},{4,5},{5,6},{6,7},{7,8},{8,9},{9,10},{10,1... | collective-permute-start | bytes 3145736 | tf_op jit(solution)/shard_map/ppermute | solution.py:16
  11.7 6.6 %collective-permute-start.1 = (bf16[1,32,32,512]{3,2,1,0:T(8,128)(2,1)S(1)}, bf16[1,32,32,512]{3,2,1,0:T(8,128)(2,1)S(1)}, u32[]{:S(2)}, u32[]{:S(2)}) collective-permute-start(bf16[1,32,32,512]{3,2,1,0:T(8,128)(2,1)S(1)} %get-tuple-element.5), channel_id=1, source_target_pairs={{1,0},{2,1},{3,2},{4,3},{5,4},{6,5},{7,6},{8,7},{9,8},{10,9},{11,1... | collective-permute-start | bytes 3145736 | tf_op jit(solution)/shard_map/ppermute | solution.py:17
  24.1 35.0 %copy-start.6 = (bf16[512,512]{1,0:T(8,128)(2,1)S(1)}, bf16[512,512]{1,0:T(8,128)(2,1)}, u32[]{:S(2)}) copy-start(bf16[512,512]{1,0:T(8,128)(2,1)} %param.11) | copy-start | bytes 1572868
  57.9 3.8 %copy-start.2 = (bf16[4,32,32,512]{3,2,1,0:T(8,128)(2,1)}, bf16[4,32,32,512]{3,2,1,0:T(8,128)(2,1)S(1)}, u32[]{:S(2)}) copy-start(bf16[4,32,32,512]{3,2,1,0:T(8,128)(2,1)S(1)} %fusion.10) | copy-start | bytes 12582916
  63.0 3.0 %copy-start.7 = (bf16[512,512]{1,0:T(8,128)(2,1)S(1)}, bf16[512,512]{1,0:T(8,128)(2,1)}, u32[]{:S(2)}) copy-start(bf16[512,512]{1,0:T(8,128)(2,1)} %param.13) | copy-start | bytes 1572868
  66.0 9.1 %copy-start.9 = (u32[32]{0:T(128)S(1)}, u32[32]{0:T(128)}, u32[]{:S(2)}) copy-start(u32[32]{0:T(128)} %constant.36) | copy-start | bytes 388
  66.0 89.4 %copy-start.3 = (bf16[512,1024]{1,0:T(8,128)(2,1)S(1)}, bf16[512,1024]{1,0:T(8,128)(2,1)}, u32[]{:S(2)}) copy-start(bf16[512,1024]{1,0:T(8,128)(2,1)} %param.15) | copy-start | bytes 3145732
  66.0 89.4 %copy-start.5 = (f32[512]{0:T(512)S(1)}, f32[512]{0:T(512)}, u32[]{:S(2)}) copy-start(f32[512]{0:T(512)} %param.14) | copy-start | bytes 6148
  66.0 111.7 %copy-start.8 = (bf16[512,512]{1,0:T(8,128)(2,1)S(1)}, bf16[512,512]{1,0:T(8,128)(2,1)}, u32[]{:S(2)}) copy-start(bf16[512,512]{1,0:T(8,128)(2,1)} %param.17) | copy-start | bytes 1572868
  156.8 29.2 %copy-start.4 = (bf16[32,512]{1,0:T(8,128)(2,1)}, bf16[32,512]{1,0:T(8,128)(2,1)S(1)}, u32[]{:S(2)}) copy-start(bf16[32,512]{1,0:T(8,128)(2,1)S(1)} %fusion.16) | copy-start | bytes 98308
Sparse Core Ops, SparseCore 0:
  75.2 78.0 reduce-scatter.1
where the time goes:
time: 193 us
  blocking collectives  70.6 us (37%)
  other arithmetic  46.7 us (24%)
  waiting for transfers between devices  29.4 us (15%)
  matrix products  22.5 us (12%)
  between operations  14.9 us (8%)
  local copies, waits for them, and re-layouts  4.62 us (2%)
  starting transfers between devices  4.06 us (2%)
    unnamed x1, blocking collectives  49.8 us
    convert_element_type x1, other arithmetic, per_device(): jax.nn.gelu(total).astype(jnp.bfloat16).reshape(-1, channels)  33.8 us
    reduce_scatter x1, waiting for transfers between devices, per_device(): lax.psum_scatter(weighted_token_share, 'gx', scatter_dimension=0, tiled=T...  27.1 us
    all_gather x1, blocking collectives, per_device(): slice_out = lax.all_gather(own_out, 'gx', axis=0, tiled=True)  20.8 us
    dot_general x1, matrix products, per_device(): lax.dot_general(slice_probs, values, (((0,), (0,)), ((), ())), preferred_...  9.05 us
    dot_general x1, matrix products, per_device(): jnp.dot(desliced, final_mapping_matrix, preferred_element_type=jnp.float32)  8.33 us
    concatenate x1, other arithmetic, padded_2(): value = jnp.concatenate([before, value, after], axis=dim)  5.76 us
  transfers between devices with their start and end apart: 3, of which 2 were waited for; matrix products, arithmetic and copies ran while one was open for 2% of the time, Pallas kernels for 0%

commit v1 on v0

v1 whole, which is shorter than its diff:
```python
import functools
import math

import jax
import jax.numpy as jnp
from jax import lax
from jax.experimental import pallas as pl
from jax.experimental.pallas import tpu as pltpu
from jax.sharding import PartitionSpec as P

epsilon = 1e-05
MESH = pl.DeviceIdType.MESH
F32 = jnp.float32
BF16 = jnp.bfloat16
LANES = 128
VMEM_LIMIT = 60 * 1024 * 1024


def gelu(v):
    a = math.sqrt(2.0 / math.pi)
    return 0.5 * v * (1.0 + jnp.tanh(v * (a + (a * 0.044715) * (v * v))))


def slab_kernel(
    plan, first, count, n_src, has_prior, last, rows_per_step, *refs
):
    refs = list(refs)
    srcs = [refs.pop(0) for _ in range(n_src)]
    taps_ref, aff_ref, soft_ref = (refs.pop(0) for _ in range(3))
    g_in = None
    if has_prior:
        refs.pop(0)
        g_in = refs.pop(0)
    p_out, g_out, pad, hid, prob, load_sem, store_sem = refs
    planes_in, rows_y2, rows_z, channels = pad.shape
    rows_y = rows_y2 - 2
    cells = rows_y * rows_z
    slices = aff_ref.shape[1]

    loads = []
    for i, (s, j) in enumerate(plan):
        copy = pltpu.make_async_copy(
            srcs[s].at[j], pad.at[i, pl.ds(1, rows_y)], load_sem.at[i]
        )
        copy.start()
        loads.append(copy)
    for i in range(planes_in):
        pad[i, 0] = jnp.zeros((rows_z, channels), BF16)
        pad[i, rows_y + 1] = jnp.zeros((rows_z, channels), BF16)
    for copy in loads:
        copy.wait()

    row = lax.broadcasted_iota(jnp.int32, (rows_z, LANES), 0)
    ones = jnp.ones((cells, LANES), BF16)
    stores = []
    for k in range(count):

        def conv_row(y, carry):
            for ch in range(channels // LANES):
                cs = pl.ds(ch * LANES, LANES)
                sums = [None, None, None]
                for a in range(3):
                    parts = [None, None, None]
                    for b in range(3):
                        v = pad[k + a, y + b, :, cs].reshape(rows_z // 16, 16, LANES)
                        for c in range(3):
                            t = v * taps_ref[9 * a + 3 * b + c, :, cs]
                            parts[c] = t if parts[c] is None else parts[c] + t
                    for c in range(3):
                        t = parts[c].astype(F32)
                        sums[c] = t if sums[c] is None else sums[c] + t
                s0, s1, s2 = (t.reshape(rows_z, LANES) for t in sums)
                total = (
                    s1
                    + jnp.where(row == 0, 0.0, pltpu.roll(s0, 1, 0))
                    + jnp.where(row == rows_z - 1, 0.0, pltpu.roll(s2, rows_z - 1, 0))
                )
                hid[pl.ds(pl.multiple_of(y * rows_z, rows_z), rows_z), cs] = gelu(
                    total
                ).astype(BF16)
            return carry

        lax.fori_loop(0, rows_y, conv_row, 0)

        def soft_step(i, carry):
            rs = pl.ds(pl.multiple_of(i * rows_per_step, rows_per_step), rows_per_step)
            h = hid[rs, :]
            logits = jnp.dot(h, aff_ref[...], preferred_element_type=F32)
            z = jnp.dot(h, soft_ref[...], preferred_element_type=F32)
            temp = 0.25 + jnp.maximum(z, 0.0) + jnp.log1p(jnp.exp(-jnp.abs(z)))
            scale = (1.0 / temp)[:, :1]
            top = jnp.max(logits, axis=-1, keepdims=True)
            e = jnp.exp((logits - top) * scale)
            e = e * (1.0 / jnp.sum(e, axis=-1, keepdims=True))
            prob[k, rs, :] = e.astype(BF16)
            return carry

        lax.fori_loop(0, cells // rows_per_step, soft_step, 0)
        store = pltpu.make_async_copy(prob.at[k], p_out.at[first + k], store_sem.at[k])
        store.start()
        stores.append(store)
        contract = (((0,), (0,)), ((), ()))
        pk = prob[k]
        g = lax.dot_general(pk, hid[...], contract, preferred_element_type=F32)
        m = lax.dot_general(pk, ones, contract, preferred_element_type=F32)
        if k == 0:
            if has_prior:
                g = g + g_in[:, :channels]
                m = m + g_in[:, channels:]
        else:
            g = g + acc_g
            m = m + acc_m
        acc_g, acc_m = g, m
    if last:
        g_out[:, :channels] = acc_g.astype(BF16)
        high = acc_m.astype(BF16).astype(F32)
        lane = lax.broadcasted_iota(jnp.int32, (slices, LANES), 1)
        g_out[:, channels:] = jnp.where(lane < LANES // 2, high, acc_m - high).astype(BF16)
    else:
        g_out[:, :channels] = acc_g
        g_out[:, channels:] = acc_m
    for store in stores:
        store.wait()


def slab(plan, first, srcs, planes, taps, aff, soft, prior, last):
    _, rows_y, rows_z, channels = srcs[0].shape
    slices = aff.shape[1]
    count = len(plan) - 2
    cells = rows_y * rows_z
    any_spec = pl.BlockSpec(memory_space=pl.ANY)
    vmem_spec = pl.BlockSpec(memory_space=pltpu.VMEM)
    args = list(srcs) + [taps, aff, soft]
    specs = [any_spec] * len(srcs) + [vmem_spec] * 3
    aliases = {}
    if prior is not None:
        aliases = {len(args): 0}
        args += list(prior)
        specs += [any_spec, vmem_spec]
    return pl.pallas_call(
        functools.partial(
            slab_kernel, plan, first, count, len(srcs), prior is not None, last, min(128, cells)
        ),
        out_shape=(
            jax.ShapeDtypeStruct((planes, cells, slices), BF16),
            jax.ShapeDtypeStruct((slices, channels + LANES), BF16 if last else F32),
        ),
        in_specs=specs,
        out_specs=(any_spec, vmem_spec),
        input_output_aliases=aliases,
        scratch_shapes=[
            pltpu.VMEM((count + 2, rows_y + 2, rows_z, channels), BF16),
            pltpu.VMEM((cells, channels), BF16),
            pltpu.VMEM((count, cells, slices), BF16),
            pltpu.SemaphoreType.DMA((count + 2,)),
            pltpu.SemaphoreType.DMA((count,)),
        ],
        compiler_params=pltpu.CompilerParams(vmem_limit_bytes=VMEM_LIMIT),
        cost_estimate=pl.CostEstimate(
            flops=count * cells * (4 * channels * slices + 200 * channels),
            bytes_accessed=count * cells * channels * 6,
            transcendentals=2 * count * cells * channels,
        ),
        name="slab_last" if last else ("slab_next" if prior is not None else "slab_first"),
    )(*args)


def exchange_kernel(
    n,
    g_ref,
    gain_ref,
    wc_hbm,
    w1_hbm,
    w2_hbm,
    wf_hbm,
    own_ref,
    all_ref,
    wc,
    w1,
    w2,
    wf,
    pair_in,
    summed,
    ring_in,
    w_sem,
    s1,
    r1,
    s2,
    r2,
    s3,
    r3,
    s4,
    r4,
):
    me = lax.axis_index("gx")
    half = n // 2
    core = lax.rem(me, 2)
    chip = me // 2
    partner = me + 1 - 2 * core
    channels = wc.shape[0]

    def there(d):
        return 2 * lax.rem(chip + d, half) + core

    def origin(d):
        return lax.rem(chip + half - d, half)

    loads = []
    for i, (src, dst) in enumerate(((wc_hbm, wc), (w1_hbm, w1), (w2_hbm, w2), (wf_hbm, wf))):
        copy = pltpu.make_async_copy(src, dst, w_sem.at[i])
        copy.start()
        loads.append(copy)

    barrier = pltpu.get_barrier_semaphore()
    pl.semaphore_signal(barrier, inc=1, device_id={"gx": partner}, device_id_type=MESH)
    for d in range(1, half):
        pl.semaphore_signal(barrier, inc=1, device_id={"gx": there(d)}, device_id_type=MESH)
    pl.semaphore_wait(barrier, half)

    def remote(src, dst, ss, rs, to):
        return pltpu.make_async_remote_copy(
            src_ref=src, dst_ref=dst, send_sem=ss, recv_sem=rs,
            device_id={"gx": to}, device_id_type=MESH,
        )

    pair = []
    for d in range(half):
        k = lax.rem(chip + (d + 1) % half, half)
        copy = remote(g_ref.at[k, 1 - core], pair_in.at[k], s1.at[d], r1.at[d], partner)
        copy.start()
        pair.append(copy)
    sends = []
    for d in range(1, half):
        k = lax.rem(chip + d, half)
        pair[d - 1].wait_recv()
        summed[k] = (g_ref[k, core].astype(F32) + pair_in[k].astype(F32)).astype(BF16)
        copy = remote(summed.at[k], ring_in.at[d], s2.at[d], r2.at[d], there(d))
        copy.start()
        sends.append(copy)
    pair[half - 1].wait_recv()
    acc = g_ref[chip, core].astype(F32) + pair_in[chip].astype(F32)
    for d in range(1, half):
        sends[d - 1].wait_recv()
        acc = acc + ring_in[d].astype(F32)
    for copy in loads:
        copy.wait()

    mass = acc[:, channels : channels + 1] + acc[
        :, channels + LANES // 2 : channels + LANES // 2 + 1
    ]
    mean_hidden = acc[:, :channels] / (mass + epsilon)
    high = mean_hidden.astype(BF16)
    low = (mean_hidden - high.astype(F32)).astype(BF16)
    tokens = jnp.dot(high, wc[...], preferred_element_type=F32) + jnp.dot(
        low, wc[...], preferred_element_type=F32
    )
    center = jnp.mean(tokens, axis=-1, keepdims=True)
    spread = jnp.mean((tokens - center) ** 2, axis=-1, keepdims=True)
    normed = ((tokens - center) * (1.0 / jnp.sqrt(spread + epsilon)) * gain_ref[...]).astype(BF16)
    inner = gelu(jnp.dot(normed, w1[...], preferred_element_type=F32)).astype(BF16)
    own = (tokens + jnp.dot(inner, w2[...], preferred_element_type=F32)).astype(BF16)
    own_ref[...] = own
    all_ref[me] = jnp.dot(own, wf[...], preferred_element_type=F32).astype(BF16)

    out = []
    for d in range(1, half):
        copy = remote(all_ref.at[me], all_ref.at[me], s3.at[d], r3.at[d], there(d))
        copy.start()
        out.append(copy)
    first = remote(all_ref.at[me], all_ref.at[me], s4.at[0], r4.at[0], partner)
    first.start()
    relays = [first]
    for d in range(1, half):
        out[d - 1].wait_recv()
        block = 2 * origin(d) + core
        copy = remote(all_ref.at[block], all_ref.at[block], s4.at[d], r4.at[d], partner)
        copy.start()
        relays.append(copy)
    for copy in pair + sends + out:
        copy.wait_send()
    for copy in relays:
        copy.wait()


def exchange(n, g, gain, wc, w1, w2, wf):
    slices, width = g.shape
    channels = wc.shape[0]
    rows, half = slices // n, n // 2
    any_spec = pl.BlockSpec(memory_space=pl.ANY)
    vmem_spec = pl.BlockSpec(memory_space=pltpu.VMEM)
    dma = pltpu.SemaphoreType.DMA
    return pl.pallas_call(
        functools.partial(exchange_kernel, n),
        out_shape=(
            jax.ShapeDtypeStruct((rows, channels), BF16),
            jax.ShapeDtypeStruct((n, rows, channels), BF16),
        ),
        in_specs=[vmem_spec, vmem_spec] + [any_spec] * 4,
        out_specs=(vmem_spec, vmem_spec),
        scratch_shapes=[
            pltpu.VMEM(wc.shape, BF16),
            pltpu.VMEM(w1.shape, BF16),
            pltpu.VMEM(w2.shape, BF16),
            pltpu.VMEM(wf.shape, BF16),
            pltpu.VMEM((half, rows, width), BF16),
            pltpu.VMEM((half, rows, width), BF16),
            pltpu.VMEM((half, rows, width), BF16),
            dma((4,)),
        ]
        + [dma((half,))] * 8,
        compiler_params=pltpu.CompilerParams(
            collective_id=0, has_side_effects=True, vmem_limit_bytes=VMEM_LIMIT
        ),
        name="exchange",
    )(g.reshape(half, 2, rows, width), gain, wc, w1, w2, wf)


def final_kernel(x_ref, p_ref, f_ref, o_ref):
    o_ref[...] = (
        x_ref[...].astype(F32) + jnp.dot(p_ref[...], f_ref[...], preferred_element_type=F32)
    ).astype(BF16)


def final(x, p, f):
    cells, channels = x.shape
    slices = p.shape[1]
    block = math.gcd(cells, 512)
    return pl.pallas_call(
        final_kernel,
        out_shape=jax.ShapeDtypeStruct((cells, channels), BF16),
        grid=(cells // block,),
        in_specs=[
            pl.BlockSpec((block, channels), lambda i: (i, 0)),
            pl.BlockSpec((block, slices), lambda i: (i, 0)),
            pl.BlockSpec((slices, channels), lambda i: (0, 0)),
        ],
        out_specs=pl.BlockSpec((block, channels), lambda i: (i, 0)),
        compiler_params=pltpu.CompilerParams(vmem_limit_bytes=VMEM_LIMIT),
        name="final",
    )(x, p, f)


def per_device(x, stencil, aff, softness, wc, gain, w1, w2, wf):
    planes, rows_y, rows_z, channels = x.shape
    n = lax.axis_size("gx")
    up = [(i, i + 1) for i in range(n - 1)]
    down = [(j, i) for i, j in up]
    before = lax.ppermute(x[planes - 1 :], "gx", up)
    after = lax.ppermute(x[:1], "gx", down)
    taps = jnp.broadcast_to(stencil.astype(BF16)[:, None, :], (27, 16, channels))
    soft = jnp.broadcast_to(softness.astype(BF16)[:, None], (channels, LANES))
    weights = (taps, aff, soft)
    prior = None
    if planes > 2:
        inside = tuple((0, j) for j in range(planes))
        prior = slab(inside, 1, (x,), planes, *weights, prior, False)
    low = ((1, 0), (0, 0), (0, 1) if planes > 1 else (2, 0))
    prior = slab(low, 0, (x, before, after), planes, *weights, prior, planes == 1)
    if planes > 1:
        high = ((0, planes - 2), (0, planes - 1), (1, 0))
        prior = slab(high, planes - 1, (x, after), planes, *weights, prior, True)
    probs, g = prior
    own, folded = exchange(n, g, gain.reshape(1, -1), wc, w1, w2, wf)
    updated = final(
        x.reshape(-1, channels),
        probs.reshape(planes * rows_y * rows_z, -1),
        folded.reshape(-1, channels),
    )
    return updated.reshape(x.shape), own


def solution(mesh):
    return jax.shard_map(
        per_device,
        mesh=mesh,
        in_specs=(P(("grp", "gx"), None, None, None), P(), P(), P(), P(), P(), P(), P(), P()),
        out_specs=(P(("grp", "gx"), None, None, None), P(("grp", "gx"), None)),
        check_vma=False,
    )
```

time: 193 us -> 103 us (0.53)
  Pallas kernels: 0 us -> 91.8 us
  blocking collectives: 70.6 us -> 0 us
  other arithmetic: 46.7 us -> 0.01 us
  waiting for transfers between devices: 29.4 us -> 0.01 us
  matrix products: 22.5 us -> 0 us
  between operations: 14.9 us -> 0.77 us
    pallas_call x0 -> x5, Pallas kernels: none -> 91.8 us  [the longest x3 56 us: slab(): pl.pallas_call(functools.partial(slab_kernel, plan, first, count, len(src...]
    unnamed x1 -> x0, blocking collectives: 49.8 us -> none
    convert_element_type x2, other arithmetic: 34.5 us -> 0.01 us  [the longest x1 0.01 us: per_device(): stencil.astype(BF16)[:, None, :]]
    reduce_scatter x1 -> x0, waiting for transfers between devices: 27.1 us -> none  [per_device(): lax.psum_scatter(weighted_token_share, 'gx', scatter_dimension=0, tiled=T...]
    dot_general x5 -> x0, matrix products: 22.5 us -> none  [the longest x1 9.05 us: per_device(): lax.dot_general(slice_probs, values, (((0,), (0,)), ((), ())), preferred_...]
    all_gather x1 -> x0, blocking collectives: 20.8 us -> none  [per_device(): slice_out = lax.all_gather(own_out, 'gx', axis=0, tiled=True)]
    reduce_sum x4 -> x0, other arithmetic: 6.35 us -> none  [the longest x1 2.96 us: per_device(): mass_part = jnp.sum(slice_probs.astype(jnp.float32), axis=0)]
    concatenate x1 -> x0, other arithmetic: 5.76 us -> none  [padded_2(): value = jnp.concatenate([before, value, after], axis=dim)]
  transfers between devices with their start and end apart: 3 -> 2, of which waited for: 2 -> 0; matrix products, arithmetic and copies ran while one was open for 2% -> 2% of each run, Pallas kernels for 0% -> 25%
where the time goes in v1:
time: 103 us
  Pallas kernels  91.8 us (89%)
  local copies, waits for them, and re-layouts  6.33 us (6%)
  starting transfers between devices  3.74 us (4%)
    pallas_call x3, Pallas kernels, slab(): pl.pallas_call(functools.partial(slab_kernel, plan, first, count, len(src...  56 us
    pallas_call x1, Pallas kernels, exchange(): pl.pallas_call(functools.partial(exchange_kernel, n), out_shape=(jax.Shap...  26.9 us
    pallas_call x1, Pallas kernels, final(): pl.pallas_call(final_kernel, out_shape=jax.ShapeDtypeStruct((cells, chann...  8.97 us
    slice x1, local copies, waits for them, and re-layouts, per_device(): before = lax.ppermute(x[planes - 1:], 'gx', up)  2.79 us
    ppermute x1, starting transfers between devices, per_device(): before = lax.ppermute(x[planes - 1:], 'gx', up)  2.45 us
  transfers between devices with their start and end apart: 2, of which 0 were waited for; matrix products, arithmetic and copies ran while one was open for 2% of the time, Pallas kernels for 25%

profile of v1, /device:TPU:0, one launch (start us, length us, event | category | flops | bytes accessed | tf_op | source)
XLA Modules:
  0.0 102.7 jit_solution(1720558790031864294)
XLA Ops:
  0.6 0.0 copy-start.4
  0.6 0.0 copy-start.2
  0.6 2.8 %fusion = (bf16[1,32,32,512]{3,2,1,0:T(8,128)(2,1)}, bf16[1,32,32,512]{3,2,1,0:T(8,128)(2,1)S(1)}) fusion(bf16[4,32,32,512]{3,2,1,0:T(8,128)(2,1)} %refs_0_.5), kind=kLoop, calls=%fused_computation | loop fusion | bytes 4194304 | tf_op jit(solution)/shard_map/slice | solution.py:348
  3.4 2.5 %collective-permute-start.1 = (bf16[1,32,32,512]{3,2,1,0:T(8,128)(2,1)}, bf16[1,32,32,512]{3,2,1,0:T(8,128)(2,1)S(1)}, u32[]{:S(2)}, u32[]{:S(2)}) collective-permute-start(bf16[1,32,32,512]{3,2,1,0:T(8,128)(2,1)} %get-tuple-element.18), channel_id=1, source_target_pairs={{0,1},{1,2},{2,3},{3,4},{4,5},{5,6},{6,7},{7,8},{8,9},{9,10},{10,1... | collective-permute-start | bytes 3145736 | tf_op jit(solution)/shard_map/ppermute | solution.py:348
  5.9 1.3 %collective-permute-start = (bf16[1,32,32,512]{3,2,1,0:T(8,128)(2,1)S(1)}, bf16[1,32,32,512]{3,2,1,0:T(8,128)(2,1)S(1)}, u32[]{:S(2)}, u32[]{:S(2)}) collective-permute-start(bf16[1,32,32,512]{3,2,1,0:T(8,128)(2,1)S(1)} %get-tuple-element.19), channel_id=1, source_target_pairs={{1,0},{2,1},{3,2},{4,3},{5,4},{6,5},{7,6},{8,7},{9,8},{10,9},{11,1... | collective-permute-start | bytes 3145736 | tf_op jit(solution)/shard_map/ppermute | solution.py:349
  7.2 0.0 copy-done.4
  7.2 0.0 copy-done.2
  7.2 0.8 broadcast_in_dim.5.refs_3_.refs_5_.refs_4_
  8.1 0.8 broadcast_in_dim.4.refs_1_.refs_3_.refs_2_
  8.9 25.7 %slab_first.1 = (bf16[4,1024,512]{2,1,0:T(8,128)(2,1)}, f32[512,640]{1,0:T(8,128)}) custom-call(bf16[4,32,32,512]{3,2,1,0:T(8,128)(2,1)} %refs_0_.5, bf16[27,16,512]{2,1,0:T(8,128)(2,1)} %broadcast_in_dim.4.refs_1_.refs_3_.refs_2_, bf16[512,512]{1,0:T(8,128)(2,1)} %refs_3_.1, bf16[512,128]{1,0:T(8,128)(2,1)} %broadcast_in_dim.5.refs_3_.refs_5_.refs_4_), custom_call_target="tpu_custom_call" | custom-call | flops 2357198848 | bytes 6291456 | tf_op jit(solution)/shard_map/slab_first/pallas_call | solution.py:140
  34.6 0.0 collective-permute-done.1.refs_1_
  34.6 0.0 copy-start.1
  34.6 0.0 collective-permute-done.refs_2_.refs_1_
  34.6 0.0 copy-start
  34.6 0.9 copy-done.1
  35.6 0.4 copy-done
  35.9 15.2 %slab_next.1 = (bf16[4,1024,512]{2,1,0:T(8,128)(2,1)}, f32[512,640]{1,0:T(8,128)}) custom-call(bf16[4,32,32,512]{3,2,1,0:T(8,128)(2,1)} %refs_0_.5, bf16[1,32,32,512]{3,2,1,0:T(8,128)(2,1)} %copy-done.1, bf16[1,32,32,512]{3,2,1,0:T(8,128)(2,1)} %copy-done, ...), custom_call_target="tpu_custom_call", output_to_operand_aliasing={{0}: (6, {})} | custom-call | flops 1178599424 | bytes 3145728 | tf_op jit(solution)/shard_map/slab_next/pallas_call | solution.py:140
  51.2 15.0 %slab_last.1 = (bf16[4,1024,512]{2,1,0:T(8,128)(2,1)}, bf16[512,640]{1,0:T(8,128)(2,1)}) custom-call(bf16[4,32,32,512]{3,2,1,0:T(8,128)(2,1)} %refs_0_.5, bf16[1,32,32,512]{3,2,1,0:T(8,128)(2,1)} %copy-done, bf16[27,16,512]{2,1,0:T(8,128)(2,1)} %broadcast_in_dim.4.refs_1_.refs_3_.refs_2_, bf16[512,512]{1,0:T(8,128)(2,1)} %refs_3_.1, ...), custom_call_target="tpu_custom_call", output_to_operand_aliasing={{0}: (5, {})} | custom-call | flops 1178599424 | bytes 3145728 | tf_op jit(solution)/shard_map/slab_last/pallas_call | solution.py:140
  66.2 26.9 %exchange.1 = (bf16[32,512]{1,0:T(8,128)(2,1)}, bf16[16,32,512]{2,1,0:T(8,128)(2,1)}) custom-call(bf16[8,2,32,640]{3,2,1,0:T(8,128)(2,1)} %bitcast.9, f32[1,512]{1,0:T(1,128)} %bitcast.11, bf16[512,512]{1,0:T(8,128)(2,1)} %wc_hbm.1, bf16[512,1024]{1,0:T(8,128)(2,1)} %w1_hbm.1, bf16[1024,512]{1,0:T(8,128)(2,1)} %w2_hbm.1, bf16[512,512]{1,0:T(8,128)(2,1)} %wf_hbm.1), custom_call_target="tpu_custom_call" | custom-call | tf_op jit(solution)/shard_map/exchange/pallas_call | solution.py:292
  93.1 0.0 copy-start.3
  93.1 9.0 %final.1 = bf16[4096,512]{1,0:T(8,128)(2,1)} custom-call(bf16[4096,512]{1,0:T(8,128)(2,1)} %bitcast.6, bf16[4096,512]{1,0:T(8,128)(2,1)} %bitcast.7, bf16[512,512]{1,0:T(8,128)(2,1)} %bitcast.10), custom_call_target="tpu_custom_call" | custom-call | tf_op jit(solution)/shard_map/final/pallas_call | solution.py:328
  102.0 0.0 copy-done.3
  102.1 0.6 copy.16
  (2 shorter events, 0.0 us)
Async XLA Ops:
  0.6 6.6 %copy-start.4 = (f32[512]{0:T(512)S(1)}, f32[512]{0:T(512)}, u32[]{:S(2)}) copy-start(f32[512]{0:T(512)} %param.12) | copy-start | bytes 6148
  0.6 6.6 %copy-start.2 = (f32[27,512]{1,0:T(8,128)S(1)}, f32[27,512]{1,0:T(8,128)}, u32[]{:S(2)}) copy-start(f32[27,512]{1,0:T(8,128)} %param.10) | copy-start | bytes 165892
  3.4 31.1 %collective-permute-start.1 = (bf16[1,32,32,512]{3,2,1,0:T(8,128)(2,1)}, bf16[1,32,32,512]{3,2,1,0:T(8,128)(2,1)S(1)}, u32[]{:S(2)}, u32[]{:S(2)}) collective-permute-start(bf16[1,32,32,512]{3,2,1,0:T(8,128)(2,1)} %get-tuple-element.18), channel_id=1, source_target_pairs={{0,1},{1,2},{2,3},{3,4},{4,5},{5,6},{6,7},{7,8},{8,9},{9,10},{10,1... | collective-permute-start | bytes 3145736 | tf_op jit(solution)/shard_map/ppermute | solution.py:348
  5.9 28.7 %collective-permute-start = (bf16[1,32,32,512]{3,2,1,0:T(8,128)(2,1)S(1)}, bf16[1,32,32,512]{3,2,1,0:T(8,128)(2,1)S(1)}, u32[]{:S(2)}, u32[]{:S(2)}) collective-permute-start(bf16[1,32,32,512]{3,2,1,0:T(8,128)(2,1)S(1)} %get-tuple-element.19), channel_id=1, source_target_pairs={{1,0},{2,1},{3,2},{4,3},{5,4},{6,5},{7,6},{8,7},{9,8},{10,9},{11,1... | collective-permute-start | bytes 3145736 | tf_op jit(solution)/shard_map/ppermute | solution.py:349
  34.6 1.0 copy-start.1
  34.6 1.3 %copy-start = (bf16[1,32,32,512]{3,2,1,0:T(8,128)(2,1)}, bf16[1,32,32,512]{3,2,1,0:T(8,128)(2,1)S(1)}, u32[]{:S(2)}) copy-start(bf16[1,32,32,512]{3,2,1,0:T(8,128)(2,1)S(1)} %collective-permute-done.refs_2_.refs_1_) | copy-start | bytes 3145732
  93.1 9.0 %copy-start.3 = (bf16[32,512]{1,0:T(8,128)(2,1)S(1)}, bf16[32,512]{1,0:T(8,128)(2,1)}, u32[]{:S(2)}) copy-start(bf16[32,512]{1,0:T(8,128)(2,1)} %get-tuple-element.23) | copy-start | bytes 98308

commit v2 on v1

--- a/solution.py
+++ b/solution.py
@@ -13,7 +13,12 @@
 F32 = jnp.float32
 BF16 = jnp.bfloat16
 LANES = 128
-VMEM_LIMIT = 60 * 1024 * 1024
+MIB = 1024 * 1024
+SLAB_LIMIT = 32 * MIB
+SMALL_LIMIT = 12 * MIB
+CONV_UNROLL = 4
+SOFT_UNROLL = 1
+STEP_ROWS = 256
 
 
 def gelu(v):
@@ -22,54 +27,106 @@
 
 
 def slab_kernel(
-    plan, first, count, n_src, has_prior, last, rows_per_step, *refs
+    n, step_rows, x_ref, taps_ref, aff_ref, soft_ref, p_out, g_out,
+    pad, hid, prob, acc, load_sem, store_sem, send_sem, recv_sem,
 ):
-    refs = list(refs)
-    srcs = [refs.pop(0) for _ in range(n_src)]
-    taps_ref, aff_ref, soft_ref = (refs.pop(0) for _ in range(3))
-    g_in = None
-    if has_prior:
-        refs.pop(0)
-        g_in = refs.pop(0)
-    p_out, g_out, pad, hid, prob, load_sem, store_sem = refs
-    planes_in, rows_y2, rows_z, channels = pad.shape
-    rows_y = rows_y2 - 2
+    planes, rows_y, rows_z, channels = x_ref.shape
     cells = rows_y * rows_z
     slices = aff_ref.shape[1]
+    me = lax.axis_index("gx")
+    inside = pl.ds(1, rows_y)
+    has_left, has_right = me > 0, me < n - 1
 
     loads = []
-    for i, (s, j) in enumerate(plan):
-        copy = pltpu.make_async_copy(
-            srcs[s].at[j], pad.at[i, pl.ds(1, rows_y)], load_sem.at[i]
-        )
+    for j in range(planes):
+        copy = pltpu.make_async_copy(x_ref.at[j], pad.at[j + 1, inside], load_sem.at[j])
         copy.start()
         loads.append(copy)
-    for i in range(planes_in):
+
+    barrier = pltpu.get_barrier_semaphore()
+
+    @pl.when(has_left)
+    def _():
+        pl.semaphore_signal(barrier, inc=1, device_id={"gx": me - 1}, device_id_type=MESH)
+
+    @pl.when(has_right)
+    def _():
+        pl.semaphore_signal(barrier, inc=1, device_id={"gx": me + 1}, device_id_type=MESH)
+
+    pl.semaphore_wait(barrier, jnp.minimum(me, 1) + jnp.minimum(n - 1 - me, 1))
+
+    up = pltpu.make_async_remote_copy(
+        src_ref=x_ref.at[planes - 1], dst_ref=pad.at[0, inside],
+        send_sem=send_sem.at[0], recv_sem=recv_sem.at[0],
+        device_id={"gx": me + 1}, device_id_type=MESH,
+    )
+    down = pltpu.make_async_remote_copy(
+        src_ref=x_ref.at[0], dst_ref=pad.at[planes + 1, inside],
+        send_sem=send_sem.at[1], recv_sem=recv_sem.at[1],
+        device_id={"gx": me - 1}, device_id_type=MESH,
+    )
+
+    @pl.when(has_right)
+    def _():
+        up.start()
+
+    @pl.when(has_left)
+    def _():
+        down.start()
+
+    for i in range(planes + 2):
         pad[i, 0] = jnp.zeros((rows_z, channels), BF16)
         pad[i, rows_y + 1] = jnp.zeros((rows_z, channels), BF16)
-    for copy in loads:
+
+    @pl.when(jnp.logical_not(has_left))
+    def _():
+        pad[0, inside] = jnp.zeros((rows_y, rows_z, channels), BF16)
+
+    @pl.when(jnp.logical_not(has_right))
+    def _():
+        pad[planes + 1, inside] = jnp.zeros((rows_y, rows_z, channels), BF16)
+
+    acc[...] = jnp.zeros_like(acc)
+    for copy in loads[:3]:
         copy.wait()
 
     row = lax.broadcasted_iota(jnp.int32, (rows_z, LANES), 0)
-    ones = jnp.ones((cells, LANES), BF16)
-    stores = []
-    for k in range(count):
-
-        def conv_row(y, carry):
-            for ch in range(channels // LANES):
-                cs = pl.ds(ch * LANES, LANES)
+
+    def plane(i, carry):
+        @pl.when(i == min(1, planes - 1))
+        def _():
+            for copy in loads[3:]:
+                copy.wait()
+
+        @pl.when(jnp.logical_and(i == max(planes - 2, 0), has_left))
+        def _():
+            up.wait_recv()
+
+        @pl.when(jnp.logical_and(i == planes - 1, has_right))
+        def _():
+            down.wait_recv()
+
+        p = jnp.where(i < planes - 2, i + 1, jnp.where(i == planes - 2, 0, planes - 1))
+
+        for ch in range(channels // LANES):
+            cs = pl.ds(ch * LANES, LANES)
+            taps = [
+                jnp.broadcast_to(taps_ref[t, :, cs], (rows_z, LANES)).astype(BF16)
+                for t in range(27)
+            ]
+
+            def conv_row(y, carry):
                 sums = [None, None, None]
                 for a in range(3):
                     parts = [None, None, None]
                     for b in range(3):
-                        v = pad[k + a, y + b, :, cs].reshape(rows_z // 16, 16, LANES)
+                        v = pad[p + a, y + b, :, cs]
                         for c in range(3):
-                            t = v * taps_ref[9 * a + 3 * b + c, :, cs]
+                            t = taps[9 * a + 3 * b + c] * v
                             parts[c] = t if parts[c] is None else parts[c] + t
                     for c in range(3):
-                        t = parts[c].astype(F32)
-                        sums[c] = t if sums[c] is None else sums[c] + t
-                s0, s1, s2 = (t.reshape(rows_z, LANES) for t in sums)
+                        sums[c] = parts[c] if sums[c] is None else sums[c] + parts[c]
+                s0, s1, s2 = (t.astype(F32) for t in sums)
                 total = (
                     s1
                     + jnp.where(row == 0, 0.0, pltpu.roll(s0, 1, 0))
@@ -78,91 +135,78 @@
                 hid[pl.ds(pl.multiple_of(y * rows_z, rows_z), rows_z), cs] = gelu(
                     total
                 ).astype(BF16)
-            return carry
-
-        lax.fori_loop(0, rows_y, conv_row, 0)
-
-        def soft_step(i, carry):
-            rs = pl.ds(pl.multiple_of(i * rows_per_step, rows_per_step), rows_per_step)
+                return carry
+
+            lax.fori_loop(0, rows_y, conv_row, 0, unroll=CONV_UNROLL)
+
+        def soft_step(j, carry):
+            rs = pl.ds(pl.multiple_of(j * step_rows, step_rows), step_rows)
             h = hid[rs, :]
             logits = jnp.dot(h, aff_ref[...], preferred_element_type=F32)
-            z = jnp.dot(h, soft_ref[...], preferred_element_type=F32)
+            z = jnp.dot(h, soft_ref[...], preferred_element_type=F32)[:, :1]
             temp = 0.25 + jnp.maximum(z, 0.0) + jnp.log1p(jnp.exp(-jnp.abs(z)))
-            scale = (1.0 / temp)[:, :1]
             top = jnp.max(logits, axis=-1, keepdims=True)
-            e = jnp.exp((logits - top) * scale)
-            e = e * (1.0 / jnp.sum(e, axis=-1, keepdims=True))
-            prob[k, rs, :] = e.astype(BF16)
+            e = jnp.exp((logits - top) * (1.0 / temp))
+            prob[p, rs, :] = (e * (1.0 / jnp.sum(e, axis=-1, keepdims=True))).astype(BF16)
             return carry
 
-        lax.fori_loop(0, cells // rows_per_step, soft_step, 0)
-        store = pltpu.make_async_copy(prob.at[k], p_out.at[first + k], store_sem.at[k])
-        store.start()
-        stores.append(store)
+        lax.fori_loop(0, cells // step_rows, soft_step, 0, unroll=SOFT_UNROLL)
+        pltpu.make_async_copy(prob.at[p], p_out.at[p], store_sem.at[p]).start()
         contract = (((0,), (0,)), ((), ()))
-        pk = prob[k]
-        g = lax.dot_general(pk, hid[...], contract, preferred_element_type=F32)
-        m = lax.dot_general(pk, ones, contract, preferred_element_type=F32)
-        if k == 0:
-            if has_prior:
-                g = g + g_in[:, :channels]
-                m = m + g_in[:, channels:]
-        else:
-            g = g + acc_g
-            m = m + acc_m
-        acc_g, acc_m = g, m
-    if last:
-        g_out[:, :channels] = acc_g.astype(BF16)
-        high = acc_m.astype(BF16).astype(F32)
-        lane = lax.broadcasted_iota(jnp.int32, (slices, LANES), 1)
-        g_out[:, channels:] = jnp.where(lane < LANES // 2, high, acc_m - high).astype(BF16)
-    else:
-        g_out[:, :channels] = acc_g
-        g_out[:, channels:] = acc_m
-    for store in stores:
-        store.wait()
-
-
-def slab(plan, first, srcs, planes, taps, aff, soft, prior, last):
-    _, rows_y, rows_z, channels = srcs[0].shape
+        pk = prob[p]
+        ones = jnp.ones((cells, LANES), BF16)
+        acc[:, :channels] += lax.dot_general(pk, hid[...], contract, preferred_element_type=F32)
+        acc[:, channels:] += lax.dot_general(pk, ones, contract, preferred_element_type=F32)
+        return carry
+
+    lax.fori_loop(0, planes, plane, 0)
+    g_out[:, :channels] = acc[:, :channels].astype(BF16)
+    mass = acc[:, channels:]
+    high = mass.astype(BF16).astype(F32)
+    lane = lax.broadcasted_iota(jnp.int32, (slices, LANES), 1)
+    g_out[:, channels:] = jnp.where(lane < LANES // 2, high, mass - high).astype(BF16)
+    for j in range(planes):
+        pltpu.make_async_copy(prob.at[j], p_out.at[j], store_sem.at[j]).wait()
+
+    @pl.when(has_right)
+    def _():
+        up.wait_send()
+
+    @pl.when(has_left)
+    def _():
+        down.wait_send()
+
+
+def slab(n, x, taps, aff, soft):
+    planes, rows_y, rows_z, channels = x.shape
     slices = aff.shape[1]
-    count = len(plan) - 2
     cells = rows_y * rows_z
     any_spec = pl.BlockSpec(memory_space=pl.ANY)
     vmem_spec = pl.BlockSpec(memory_space=pltpu.VMEM)
-    args = list(srcs) + [taps, aff, soft]
-    specs = [any_spec] * len(srcs) + [vmem_spec] * 3
-    aliases = {}
-    if prior is not None:
-        aliases = {len(args): 0}
-        args += list(prior)
-        specs += [any_spec, vmem_spec]
+    dma = pltpu.SemaphoreType.DMA
     return pl.pallas_call(
-        functools.partial(
-            slab_kernel, plan, first, count, len(srcs), prior is not None, last, min(128, cells)
-        ),
+        functools.partial(slab_kernel, n, min(STEP_ROWS, cells)),
         out_shape=(
             jax.ShapeDtypeStruct((planes, cells, slices), BF16),
-            jax.ShapeDtypeStruct((slices, channels + LANES), BF16 if last else F32),
+            jax.ShapeDtypeStruct((slices, channels + LANES), BF16),
         ),
-        in_specs=specs,
+        in_specs=[pl.BlockSpec(memory_space=pltpu.HBM)] + [vmem_spec] * 3,
         out_specs=(any_spec, vmem_spec),
-        input_output_aliases=aliases,
         scratch_shapes=[
-            pltpu.VMEM((count + 2, rows_y + 2, rows_z, channels), BF16),
+            pltpu.VMEM((planes + 2, rows_y + 2, rows_z, channels), BF16),
             pltpu.VMEM((cells, channels), BF16),
-            pltpu.VMEM((count, cells, slices), BF16),
-            pltpu.SemaphoreType.DMA((count + 2,)),
-            pltpu.SemaphoreType.DMA((count,)),
+            pltpu.VMEM((planes, cells, slices), BF16),
+            pltpu.VMEM((slices, channels + LANES), F32),
+            dma((planes,)),
+            dma((planes,)),
+            dma((2,)),
+            dma((2,)),
         ],
-        compiler_params=pltpu.CompilerParams(vmem_limit_bytes=VMEM_LIMIT),
-        cost_estimate=pl.CostEstimate(
-            flops=count * cells * (4 * channels * slices + 200 * channels),
-            bytes_accessed=count * cells * channels * 6,
-            transcendentals=2 * count * cells * channels,
+        compiler_params=pltpu.CompilerParams(
+            collective_id=1, has_side_effects=True, vmem_limit_bytes=SLAB_LIMIT
         ),
-        name="slab_last" if last else ("slab_next" if prior is not None else "slab_first"),
-    )(*args)
+        name="slab",
+    )(x, taps, aff, soft)
 
 
 def exchange_kernel(
@@ -309,7 +353,7 @@
         ]
         + [dma((half,))] * 8,
         compiler_params=pltpu.CompilerParams(
-            collective_id=0, has_side_effects=True, vmem_limit_bytes=VMEM_LIMIT
+            collective_id=0, has_side_effects=True, vmem_limit_bytes=SMALL_LIMIT
         ),
         name="exchange",
     )(g.reshape(half, 2, rows, width), gain, wc, w1, w2, wf)
@@ -335,7 +379,7 @@
             pl.BlockSpec((slices, channels), lambda i: (0, 0)),
         ],
         out_specs=pl.BlockSpec((block, channels), lambda i: (i, 0)),
-        compiler_params=pltpu.CompilerParams(vmem_limit_bytes=VMEM_LIMIT),
+        compiler_params=pltpu.CompilerParams(vmem_limit_bytes=SMALL_LIMIT),
         name="final",
     )(x, p, f)
 
@@ -343,23 +387,8 @@
 def per_device(x, stencil, aff, softness, wc, gain, w1, w2, wf):
     planes, rows_y, rows_z, channels = x.shape
     n = lax.axis_size("gx")
-    up = [(i, i + 1) for i in range(n - 1)]
-    down = [(j, i) for i, j in up]
-    before = lax.ppermute(x[planes - 1 :], "gx", up)
-    after = lax.ppermute(x[:1], "gx", down)
-    taps = jnp.broadcast_to(stencil.astype(BF16)[:, None, :], (27, 16, channels))
     soft = jnp.broadcast_to(softness.astype(BF16)[:, None], (channels, LANES))
-    weights = (taps, aff, soft)
-    prior = None
-    if planes > 2:
-        inside = tuple((0, j) for j in range(planes))
-        prior = slab(inside, 1, (x,), planes, *weights, prior, False)
-    low = ((1, 0), (0, 0), (0, 1) if planes > 1 else (2, 0))
-    prior = slab(low, 0, (x, before, after), planes, *weights, prior, planes == 1)
-    if planes > 1:
-        high = ((0, planes - 2), (0, planes - 1), (1, 0))
-        prior = slab(high, planes - 1, (x, after), planes, *weights, prior, True)
-    probs, g = prior
+    probs, g = slab(n, x, stencil[:, None, :], aff, soft)
     own, folded = exchange(n, g, gain.reshape(1, -1), wc, w1, w2, wf)
     updated = final(
         x.reshape(-1, channels),

time: 103 us -> 74.6 us (0.72)
  Pallas kernels: 91.8 us -> 67.8 us
  starting transfers between devices: 3.74 us -> 0 us
  local copies, waits for them, and re-layouts: 6.33 us -> 4.86 us
    pallas_call x3 -> x1, Pallas kernels: 56 us -> 29.3 us  [slab(): pl.pallas_call(functools.partial(slab_kernel, n, min(STEP_ROWS, cells)),...]
    pallas_call x1, Pallas kernels: 26.9 us -> 33.2 us  [exchange(): pl.pallas_call(functools.partial(exchange_kernel, n), out_shape=(jax.Shap...]
    ppermute x2 -> x0, starting transfers between devices: 3.74 us -> none  [the longest x1 2.45 us: per_device(): before = lax.ppermute(x[planes - 1:], 'gx', up)]
    pallas_call x1, Pallas kernels: 8.97 us -> 5.39 us  [final(): pl.pallas_call(final_kernel, out_shape=jax.ShapeDtypeStruct((cells, chann...]
    slice x1 -> x0, local copies, waits for them, and re-layouts: 2.79 us -> none  [per_device(): before = lax.ppermute(x[planes - 1:], 'gx', up)]
    unnamed x11 -> x15, local copies, waits for them, and re-layouts: 1.93 us -> 3.86 us
  transfers between devices with their start and end apart: 2 -> 0, of which waited for: 0 -> 0; matrix products, arithmetic and copies ran while one was open for 2% -> 0% of each run, Pallas kernels for 25% -> 0%
where the time goes in v2:
time: 74.6 us; the launch traced here: 74.1 us
  Pallas kernels  67.8 us (91%)
  local copies, waits for them, and re-layouts  4.86 us (7%)
    pallas_call x1, Pallas kernels, exchange(): pl.pallas_call(functools.partial(exchange_kernel, n), out_shape=(jax.Shap...  33.2 us
    pallas_call x1, Pallas kernels, slab(): pl.pallas_call(functools.partial(slab_kernel, n, min(STEP_ROWS, cells)),...  29.3 us
    pallas_call x1, Pallas kernels, final(): pl.pallas_call(final_kernel, out_shape=jax.ShapeDtypeStruct((cells, chann...  5.39 us
    unnamed x15, local copies, waits for them, and re-layouts  3.86 us

profile of v2, /device:TPU:0, one launch (start us, length us, event | category | flops | bytes accessed | tf_op | source)
XLA Modules:
  0.0 74.1 jit_solution(7798876093883843568)
XLA Ops:
  0.6 0.0 copy-start.6
  0.6 0.7 convert_element_type.3
  1.3 0.9 %broadcast_in_dim.4.taps_ref = f32[27,1,512]{2,1,0:T(1,128)S(1)} reshape(f32[27,512]{1,0:T(8,128)} %param.10) | data formatting | bytes 110592 | tf_op jit(solution)/shard_map/broadcast_in_dim | solution.py:391
  2.2 0.1 broadcast_in_dim.10.soft_ref
  2.3 0.0 copy-start
  2.4 2.2 %copy-done = bf16[4,32,32,512]{3,2,1,0:T(8,128)(2,1)S(1)} copy-done((bf16[4,32,32,512]{3,2,1,0:T(8,128)(2,1)S(1)}, bf16[4,32,32,512]{3,2,1,0:T(8,128)(2,1)}, u32[]{:S(2)}) %copy-start) | copy-done | bytes 4194328
  4.5 0.0 copy-start.3
  4.5 1.0 %copy-done.3 = bf16[512,512]{1,0:T(8,128)(2,1)S(1)} copy-done((bf16[512,512]{1,0:T(8,128)(2,1)S(1)}, bf16[512,512]{1,0:T(8,128)(2,1)}, u32[]{:S(2)}) %copy-start.3) | copy-done | bytes 524312
  5.6 0.0 copy-start.1
  5.6 0.0 copy-start.2
  5.6 0.0 copy-start.4
  5.6 0.0 copy-start.5
  5.6 29.3 %slab.1 = (bf16[4,1024,512]{2,1,0:T(8,128)(2,1)S(1)}, bf16[512,640]{1,0:T(8,128)(2,1)S(1)}) custom-call(bf16[4,32,32,512]{3,2,1,0:T(8,128)(2,1)S(1)} %copy-done, f32[27,1,512]{2,1,0:T(1,128)S(1)} %broadcast_in_dim.4.taps_ref, bf16[512,512]{1,0:T(8,128)(2,1)S(1)} %copy-done.3, bf16[512,128]{1,0:T(8,128)(2,1)S(1)} %broadcast_in_dim.10.soft_ref), custom_call_target="tpu_custom_call" | custom-call | tf_op jit(solution)/shard_map/slab/pallas_call | solution.py:187
  34.9 0.0 copy-done.6
  34.9 0.0 copy-done.1
  34.9 0.0 copy-done.2
  34.9 0.0 copy-done.4
  34.9 0.0 copy-done.5
  34.9 33.2 %exchange.1 = (bf16[32,512]{1,0:T(8,128)(2,1)S(1)}, bf16[16,32,512]{2,1,0:T(8,128)(2,1)S(1)}) custom-call(bf16[8,2,32,640]{3,2,1,0:T(8,128)(2,1)S(1)} %bitcast.8, f32[1,512]{1,0:T(1,128)S(1)} %bitcast.10, bf16[512,512]{1,0:T(8,128)(2,1)S(1)} %copy-done.4, bf16[512,1024]{1,0:T(8,128)(2,1)S(1)} %copy-done.1, bf16[1024,512]{1,0:T(8,128)(2,1)S(1)} %copy-done.2, ...), custom_call_target="tpu_custom_call" | custom-call | tf_op jit(solution)/shard_map/exchange/pallas_call | solution.py:336
  68.1 5.4 %final.1 = bf16[4096,512]{1,0:T(8,128)(2,1)} custom-call(bf16[4096,512]{1,0:T(8,128)(2,1)S(1)} %bitcast.6, bf16[4096,512]{1,0:T(8,128)(2,1)S(1)} %bitcast.7, bf16[512,512]{1,0:T(8,128)(2,1)S(1)} %bitcast.9), custom_call_target="tpu_custom_call" | custom-call | tf_op jit(solution)/shard_map/final/pallas_call | solution.py:372
  73.5 0.6 copy.12
Async XLA Ops:
  0.6 34.2 %copy-start.6 = (f32[512]{0:T(512)S(1)}, f32[512]{0:T(512)}, u32[]{:S(2)}) copy-start(f32[512]{0:T(512)} %param.14) | copy-start | bytes 6148
  2.3 2.2 %copy-start = (bf16[4,32,32,512]{3,2,1,0:T(8,128)(2,1)S(1)}, bf16[4,32,32,512]{3,2,1,0:T(8,128)(2,1)}, u32[]{:S(2)}) copy-start(bf16[4,32,32,512]{3,2,1,0:T(8,128)(2,1)} %x_ref.1) | copy-start | bytes 12582916
  4.5 1.0 %copy-start.3 = (bf16[512,512]{1,0:T(8,128)(2,1)S(1)}, bf16[512,512]{1,0:T(8,128)(2,1)}, u32[]{:S(2)}) copy-start(bf16[512,512]{1,0:T(8,128)(2,1)} %aff_ref.1) | copy-start | bytes 1572868
  5.6 29.3 %copy-start.1 = (bf16[512,1024]{1,0:T(8,128)(2,1)S(1)}, bf16[512,1024]{1,0:T(8,128)(2,1)}, u32[]{:S(2)}) copy-start(bf16[512,1024]{1,0:T(8,128)(2,1)} %w1_hbm.1) | copy-start | bytes 3145732
  5.6 29.3 %copy-start.2 = (bf16[1024,512]{1,0:T(8,128)(2,1)S(1)}, bf16[1024,512]{1,0:T(8,128)(2,1)}, u32[]{:S(2)}) copy-start(bf16[1024,512]{1,0:T(8,128)(2,1)} %w2_hbm.1) | copy-start | bytes 3145732
  5.6 29.3 %copy-start.4 = (bf16[512,512]{1,0:T(8,128)(2,1)S(1)}, bf16[512,512]{1,0:T(8,128)(2,1)}, u32[]{:S(2)}) copy-start(bf16[512,512]{1,0:T(8,128)(2,1)} %wc_hbm.1) | copy-start | bytes 1572868
  5.6 29.3 %copy-start.5 = (bf16[512,512]{1,0:T(8,128)(2,1)S(1)}, bf16[512,512]{1,0:T(8,128)(2,1)}, u32[]{:S(2)}) copy-start(bf16[512,512]{1,0:T(8,128)(2,1)} %wf_hbm.1) | copy-start | bytes 1572868

commit v3 on v2

--- a/solution.py
+++ b/solution.py
@@ -27,8 +27,9 @@
 
 
 def slab_kernel(
-    n, step_rows, x_ref, taps_ref, aff_ref, soft_ref, p_out, g_out,
-    pad, hid, prob, acc, load_sem, store_sem, send_sem, recv_sem,
+    n, step_rows, x_ref, taps_hbm, aff_hbm, soft_hbm, p_out, g_out,
+    taps_ref, aff_ref, soft_ref, pad, hid, prob, acc,
+    load_sem, small_sem, store_sem, send_sem, recv_sem,
 ):
     planes, rows_y, rows_z, channels = x_ref.shape
     cells = rows_y * rows_z
@@ -36,7 +37,15 @@
     me = lax.axis_index("gx")
     inside = pl.ds(1, rows_y)
     has_left, has_right = me > 0, me < n - 1
-
+    core, early = lax.rem(me, 2), max(planes - 2, 0)
+
+    small = []
+    for i, (src, dst) in enumerate(
+        ((taps_hbm, taps_ref), (aff_hbm, aff_ref), (soft_hbm, soft_ref))
+    ):
+        copy = pltpu.make_async_copy(src, dst, small_sem.at[i])
+        copy.start()
+        small.append(copy)
     loads = []
     for j in range(planes):
         copy = pltpu.make_async_copy(x_ref.at[j], pad.at[j + 1, inside], load_sem.at[j])
@@ -87,10 +96,11 @@
         pad[planes + 1, inside] = jnp.zeros((rows_y, rows_z, channels), BF16)
 
     acc[...] = jnp.zeros_like(acc)
-    for copy in loads[:3]:
+    for copy in loads[:3] + small:
         copy.wait()
 
     row = lax.broadcasted_iota(jnp.int32, (rows_z, LANES), 0)
+    soft = jnp.broadcast_to(soft_ref[...].astype(BF16), (LANES, channels))
 
     def plane(i, carry):
         @pl.when(i == min(1, planes - 1))
@@ -98,20 +108,20 @@
             for copy in loads[3:]:
                 copy.wait()
 
-        @pl.when(jnp.logical_and(i == max(planes - 2, 0), has_left))
+        @pl.when(jnp.logical_and(i == jnp.where(core == 0, planes - 1, early), has_left))
         def _():
             up.wait_recv()
 
-        @pl.when(jnp.logical_and(i == planes - 1, has_right))
+        @pl.when(jnp.logical_and(i == jnp.where(core == 0, early, planes - 1), has_right))
         def _():
             down.wait_recv()
 
-        p = jnp.where(i < planes - 2, i + 1, jnp.where(i == planes - 2, 0, planes - 1))
+        p = jnp.where(i < planes - 2, i + 1, jnp.where((i == planes - 1) == (core == 0), 0, planes - 1))
 
         for ch in range(channels // LANES):
             cs = pl.ds(ch * LANES, LANES)
             taps = [
-                jnp.broadcast_to(taps_ref[t, :, cs], (rows_z, LANES)).astype(BF16)
+                jnp.broadcast_to(taps_ref[t : t + 1, cs], (rows_z, LANES)).astype(BF16)
                 for t in range(27)
             ]
 
@@ -143,7 +153,7 @@
             rs = pl.ds(pl.multiple_of(j * step_rows, step_rows), step_rows)
             h = hid[rs, :]
             logits = jnp.dot(h, aff_ref[...], preferred_element_type=F32)
-            z = jnp.dot(h, soft_ref[...], preferred_element_type=F32)[:, :1]
+            z = lax.dot_general(h, soft, (((1,), (1,)), ((), ())), preferred_element_type=F32)[:, :1]
             temp = 0.25 + jnp.maximum(z, 0.0) + jnp.log1p(jnp.exp(-jnp.abs(z)))
             top = jnp.max(logits, axis=-1, keepdims=True)
             e = jnp.exp((logits - top) * (1.0 / temp))
@@ -190,14 +200,18 @@
             jax.ShapeDtypeStruct((planes, cells, slices), BF16),
             jax.ShapeDtypeStruct((slices, channels + LANES), BF16),
         ),
-        in_specs=[pl.BlockSpec(memory_space=pltpu.HBM)] + [vmem_spec] * 3,
+        in_specs=[pl.BlockSpec(memory_space=pltpu.HBM)] * 4,
         out_specs=(any_spec, vmem_spec),
         scratch_shapes=[
+            pltpu.VMEM(taps.shape, F32),
+            pltpu.VMEM(aff.shape, BF16),
+            pltpu.VMEM(soft.shape, F32),
             pltpu.VMEM((planes + 2, rows_y + 2, rows_z, channels), BF16),
             pltpu.VMEM((cells, channels), BF16),
             pltpu.VMEM((planes, cells, slices), BF16),
             pltpu.VMEM((slices, channels + LANES), F32),
             dma((planes,)),
+            dma((3,)),
             dma((planes,)),
             dma((2,)),
             dma((2,)),
@@ -212,13 +226,14 @@
 def exchange_kernel(
     n,
     g_ref,
-    gain_ref,
+    gain_hbm,
     wc_hbm,
     w1_hbm,
     w2_hbm,
     wf_hbm,
     own_ref,
     all_ref,
+    gain_ref,
     wc,
     w1,
     w2,
@@ -250,7 +265,9 @@
         return lax.rem(chip + half - d, half)
 
     loads = []
-    for i, (src, dst) in enumerate(((wc_hbm, wc), (w1_hbm, w1), (w2_hbm, w2), (wf_hbm, wf))):
+    for i, (src, dst) in enumerate(
+        ((wc_hbm, wc), (w1_hbm, w1), (w2_hbm, w2), (wf_hbm, wf), (gain_hbm, gain_ref))
+    ):
         copy = pltpu.make_async_copy(src, dst, w_sem.at[i])
         copy.start()
         loads.append(copy)
@@ -330,7 +347,6 @@
     slices, width = g.shape
     channels = wc.shape[0]
     rows, half = slices // n, n // 2
-    any_spec = pl.BlockSpec(memory_space=pl.ANY)
     vmem_spec = pl.BlockSpec(memory_space=pltpu.VMEM)
     dma = pltpu.SemaphoreType.DMA
     return pl.pallas_call(
@@ -339,9 +355,10 @@
             jax.ShapeDtypeStruct((rows, channels), BF16),
             jax.ShapeDtypeStruct((n, rows, channels), BF16),
         ),
-        in_specs=[vmem_spec, vmem_spec] + [any_spec] * 4,
+        in_specs=[vmem_spec] + [pl.BlockSpec(memory_space=pltpu.HBM)] * 5,
         out_specs=(vmem_spec, vmem_spec),
         scratch_shapes=[
+            pltpu.VMEM(gain.shape, F32),
             pltpu.VMEM(wc.shape, BF16),
             pltpu.VMEM(w1.shape, BF16),
             pltpu.VMEM(w2.shape, BF16),
@@ -349,7 +366,7 @@
             pltpu.VMEM((half, rows, width), BF16),
             pltpu.VMEM((half, rows, width), BF16),
             pltpu.VMEM((half, rows, width), BF16),
-            dma((4,)),
+            dma((5,)),
         ]
         + [dma((half,))] * 8,
         compiler_params=pltpu.CompilerParams(
@@ -359,41 +376,54 @@
     )(g.reshape(half, 2, rows, width), gain, wc, w1, w2, wf)
 
 
-def final_kernel(x_ref, p_ref, f_ref, o_ref):
+def final_kernel(x_ref, p_ref, f_ref, own_ref, o_ref, own_out):
+    own_out[...] = own_ref[...]
     o_ref[...] = (
         x_ref[...].astype(F32) + jnp.dot(p_ref[...], f_ref[...], preferred_element_type=F32)
     ).astype(BF16)
 
 
-def final(x, p, f):
+def final(x, p, f, own):
     cells, channels = x.shape
     slices = p.shape[1]
     block = math.gcd(cells, 512)
     return pl.pallas_call(
         final_kernel,
-        out_shape=jax.ShapeDtypeStruct((cells, channels), BF16),
+        out_shape=(
+            jax.ShapeDtypeStruct((cells, channels), BF16),
+            jax.ShapeDtypeStruct(own.shape, BF16),
+        ),
         grid=(cells // block,),
         in_specs=[
             pl.BlockSpec((block, channels), lambda i: (i, 0)),
             pl.BlockSpec((block, slices), lambda i: (i, 0)),
             pl.BlockSpec((slices, channels), lambda i: (0, 0)),
+            pl.BlockSpec(own.shape, lambda i: (0, 0)),
         ],
-        out_specs=pl.BlockSpec((block, channels), lambda i: (i, 0)),
+        out_specs=(
+            pl.BlockSpec((block, channels), lambda i: (i, 0)),
+            pl.BlockSpec(own.shape, lambda i: (0, 0)),
+        ),
         compiler_params=pltpu.CompilerParams(vmem_limit_bytes=SMALL_LIMIT),
         name="final",
-    )(x, p, f)
+    )(x, p, f, own)
 
 
 def per_device(x, stencil, aff, softness, wc, gain, w1, w2, wf):
     planes, rows_y, rows_z, channels = x.shape
     n = lax.axis_size("gx")
-    soft = jnp.broadcast_to(softness.astype(BF16)[:, None], (channels, LANES))
-    probs, g = slab(n, x, stencil[:, None, :], aff, soft)
-    own, folded = exchange(n, g, gain.reshape(1, -1), wc, w1, w2, wf)
-    updated = final(
+    def held(v):
+        return pltpu.with_memory_space_constraint(v, pltpu.HBM)
+
+    probs, g = slab(n, held(x), held(stencil), held(aff), held(softness.reshape(1, -1)))
+    own, folded = exchange(
+        n, g, held(gain.reshape(1, -1)), held(wc), held(w1), held(w2), held(wf)
+    )
+    updated, own = final(
         x.reshape(-1, channels),
         probs.reshape(planes * rows_y * rows_z, -1),
         folded.reshape(-1, channels),
+        own,
     )
     return updated.reshape(x.shape), own
 

time: 74.6 us -> 64 us (0.86)
  local copies, waits for them, and re-layouts: 4.86 us -> 0.01 us
  Pallas kernels: 67.8 us -> 63 us
    pallas_call x1, Pallas kernels: 33.2 us -> 23.7 us  [exchange(): pl.pallas_call(functools.partial(exchange_kernel, n), out_shape=(jax.Shap...]
    pallas_call x1, Pallas kernels: 29.3 us -> 33.9 us  [slab(): pl.pallas_call(functools.partial(slab_kernel, n, min(STEP_ROWS, cells)),...]
    unnamed x15 -> x2, local copies, waits for them, and re-layouts: 3.86 us -> 0.01 us
    broadcast_in_dim x2 -> x0, local copies, waits for them, and re-layouts: 1.01 us -> none  [the longest x1 0.88 us: per_device(): probs, g = slab(n, x, stencil[:, None, :], aff, soft)]
where the time goes in v3:
time: 64 us; the launch traced here: 63.7 us
  Pallas kernels  63 us (98%)
  between operations  0.66 us (1%)
    pallas_call x1, Pallas kernels, slab(): pl.pallas_call(functools.partial(slab_kernel, n, min(STEP_ROWS, cells)),...  33.9 us
    pallas_call x1, Pallas kernels, exchange(): pl.pallas_call(functools.partial(exchange_kernel, n), out_shape=(jax.Shap...  23.7 us
    pallas_call x1, Pallas kernels, final(): pl.pallas_call(final_kernel, out_shape=(jax.ShapeDtypeStruct((cells, chan...  5.4 us

profile of v3, /device:TPU:0, one launch (start us, length us, event | category | flops | bytes accessed | tf_op | source)
XLA Modules:
  0.0 63.7 jit_solution(4116192484884794916)
XLA Ops:
  0.6 0.0 copy-start
  0.6 33.9 %slab.1 = (bf16[4,1024,512]{2,1,0:T(8,128)(2,1)S(1)}, bf16[512,640]{1,0:T(8,128)(2,1)S(1)}) custom-call(bf16[4,32,32,512]{3,2,1,0:T(8,128)(2,1)} %x_ref.1, f32[27,512]{1,0:T(8,128)} %taps_hbm.1, bf16[512,512]{1,0:T(8,128)(2,1)} %aff_hbm.1, f32[1,512]{1,0:T(1,128)} %bitcast.12), custom_call_target="tpu_custom_call" | custom-call | tf_op jit(solution)/shard_map/slab/pallas_call | solution.py:197
  34.6 23.7 %exchange.1 = (bf16[32,512]{1,0:T(8,128)(2,1)S(1)}, bf16[16,32,512]{2,1,0:T(8,128)(2,1)S(1)}) custom-call(bf16[8,2,32,640]{3,2,1,0:T(8,128)(2,1)S(1)} %bitcast.9, f32[1,512]{1,0:T(1,128)} %bitcast.11, bf16[512,512]{1,0:T(8,128)(2,1)} %wc_hbm.1, bf16[512,1024]{1,0:T(8,128)(2,1)} %w1_hbm.1, bf16[1024,512]{1,0:T(8,128)(2,1)} %w2_hbm.1, bf16[512,512]{1,0:T(8,128)(2,1)} %wf_hbm.1), custom_call_target="tpu_custom_call" | custom-call | tf_op jit(solution)/shard_map/exchange/pallas_call | solution.py:352
  58.3 0.0 copy-done
  58.3 5.4 %final.1 = (bf16[4096,512]{1,0:T(8,128)(2,1)}, bf16[32,512]{1,0:T(8,128)(2,1)}) custom-call(bf16[4096,512]{1,0:T(8,128)(2,1)S(1)} %bitcast.7, bf16[4096,512]{1,0:T(8,128)(2,1)S(1)} %bitcast.8, bf16[512,512]{1,0:T(8,128)(2,1)S(1)} %bitcast.10, bf16[32,512]{1,0:T(8,128)(2,1)S(1)} %get-tuple-element.11.own_ref), custom_call_target="tpu_custom_call" | custom-call | tf_op jit(solution)/shard_map/final/pallas_call | solution.py:390
Async XLA Ops:
  0.6 57.7 %copy-start = (bf16[4,32,32,512]{3,2,1,0:T(8,128)(2,1)S(1)}, bf16[4,32,32,512]{3,2,1,0:T(8,128)(2,1)}, u32[]{:S(2)}) copy-start(bf16[4,32,32,512]{3,2,1,0:T(8,128)(2,1)} %x_ref.1) | copy-start | bytes 12582916

commit v4 on v3

--- a/solution.py
+++ b/solution.py
@@ -16,7 +16,7 @@
 MIB = 1024 * 1024
 SLAB_LIMIT = 32 * MIB
 SMALL_LIMIT = 12 * MIB
-CONV_UNROLL = 4
+CONV_UNROLL = 8
 SOFT_UNROLL = 1
 STEP_ROWS = 256
 
@@ -376,34 +376,42 @@
     )(g.reshape(half, 2, rows, width), gain, wc, w1, w2, wf)
 
 
-def final_kernel(x_ref, p_ref, f_ref, own_ref, o_ref, own_out):
+def final_kernel(x_ref, p_ref, f_ref, own_ref, o_hbm, own_out, buf, sem):
     own_out[...] = own_ref[...]
-    o_ref[...] = (
-        x_ref[...].astype(F32) + jnp.dot(p_ref[...], f_ref[...], preferred_element_type=F32)
-    ).astype(BF16)
+    slots, block, _ = buf.shape
+    steps = x_ref.shape[0] // block
+    out = []
+    for i in range(steps):
+        rs = pl.ds(i * block, block)
+        if i >= slots:
+            out[i - slots].wait()
+        buf[i % slots] = (
+            x_ref[rs, :].astype(F32)
+            + jnp.dot(p_ref[rs, :], f_ref[...], preferred_element_type=F32)
+        ).astype(BF16)
+        copy = pltpu.make_async_copy(buf.at[i % slots], o_hbm.at[rs, :], sem.at[i % slots])
+        copy.start()
+        out.append(copy)
+    for copy in out[max(steps - slots, 0) :]:
+        copy.wait()
 
 
 def final(x, p, f, own):
     cells, channels = x.shape
-    slices = p.shape[1]
     block = math.gcd(cells, 512)
+    vmem_spec = pl.BlockSpec(memory_space=pltpu.VMEM)
     return pl.pallas_call(
         final_kernel,
         out_shape=(
             jax.ShapeDtypeStruct((cells, channels), BF16),
             jax.ShapeDtypeStruct(own.shape, BF16),
         ),
-        grid=(cells // block,),
-        in_specs=[
-            pl.BlockSpec((block, channels), lambda i: (i, 0)),
-            pl.BlockSpec((block, slices), lambda i: (i, 0)),
-            pl.BlockSpec((slices, channels), lambda i: (0, 0)),
-            pl.BlockSpec(own.shape, lambda i: (0, 0)),
+        in_specs=[vmem_spec] * 4,
+        out_specs=(pl.BlockSpec(memory_space=pl.ANY), vmem_spec),
+        scratch_shapes=[
+            pltpu.VMEM((3, block, channels), BF16),
+            pltpu.SemaphoreType.DMA((3,)),
         ],
-        out_specs=(
-            pl.BlockSpec((block, channels), lambda i: (i, 0)),
-            pl.BlockSpec(own.shape, lambda i: (0, 0)),
-        ),
         compiler_params=pltpu.CompilerParams(vmem_limit_bytes=SMALL_LIMIT),
         name="final",
     )(x, p, f, own)

time: 64 us -> 62.6 us (0.978)
  Pallas kernels: 63 us -> 61.7 us
    pallas_call x1, Pallas kernels: 33.9 us -> 33.1 us  [slab(): pl.pallas_call(functools.partial(slab_kernel, n, min(STEP_ROWS, cells)),...]
where the time goes in v4:
time: 62.6 us; the launch traced here: 62.3 us
  Pallas kernels  61.7 us (99%)
  between operations  0.66 us (1%)
    pallas_call x1, Pallas kernels, slab(): pl.pallas_call(functools.partial(slab_kernel, n, min(STEP_ROWS, cells)),...  33.1 us
    pallas_call x1, Pallas kernels, exchange(): pl.pallas_call(functools.partial(exchange_kernel, n), out_shape=(jax.Shap...  23.7 us
    pallas_call x1, Pallas kernels, final(): pl.pallas_call(final_kernel, out_shape=(jax.ShapeDtypeStruct((cells, chan...  4.88 us

profile of v4, /device:TPU:0, one launch (start us, length us, event | category | flops | bytes accessed | tf_op | source)
XLA Modules:
  0.0 62.3 jit_solution(11739765350750299551)
XLA Ops:
  0.6 0.0 copy-start
  0.6 33.1 %slab.1 = (bf16[4,1024,512]{2,1,0:T(8,128)(2,1)S(1)}, bf16[512,640]{1,0:T(8,128)(2,1)S(1)}) custom-call(bf16[4,32,32,512]{3,2,1,0:T(8,128)(2,1)} %x_ref.1, f32[27,512]{1,0:T(8,128)} %taps_hbm.1, bf16[512,512]{1,0:T(8,128)(2,1)} %aff_hbm.1, f32[1,512]{1,0:T(1,128)} %bitcast.12), custom_call_target="tpu_custom_call" | custom-call | tf_op jit(solution)/shard_map/slab/pallas_call | solution.py:197
  33.7 23.7 %exchange.1 = (bf16[32,512]{1,0:T(8,128)(2,1)S(1)}, bf16[16,32,512]{2,1,0:T(8,128)(2,1)S(1)}) custom-call(bf16[8,2,32,640]{3,2,1,0:T(8,128)(2,1)S(1)} %bitcast.9, f32[1,512]{1,0:T(1,128)} %bitcast.11, bf16[512,512]{1,0:T(8,128)(2,1)} %wc_hbm.1, bf16[512,1024]{1,0:T(8,128)(2,1)} %w1_hbm.1, bf16[1024,512]{1,0:T(8,128)(2,1)} %w2_hbm.1, bf16[512,512]{1,0:T(8,128)(2,1)} %wf_hbm.1), custom_call_target="tpu_custom_call" | custom-call | tf_op jit(solution)/shard_map/exchange/pallas_call | solution.py:352
  57.4 0.0 copy-done
  57.4 4.9 %final.1 = (bf16[4096,512]{1,0:T(8,128)(2,1)}, bf16[32,512]{1,0:T(8,128)(2,1)}) custom-call(bf16[4096,512]{1,0:T(8,128)(2,1)S(1)} %bitcast.7, bf16[4096,512]{1,0:T(8,128)(2,1)S(1)} %bitcast.8, bf16[512,512]{1,0:T(8,128)(2,1)S(1)} %bitcast.10, bf16[32,512]{1,0:T(8,128)(2,1)S(1)} %get-tuple-element.11.own_ref), custom_call_target="tpu_custom_call" | custom-call | tf_op jit(solution)/shard_map/final/pallas_call | solution.py:403
Async XLA Ops:
  0.6 56.8 %copy-start = (bf16[4,32,32,512]{3,2,1,0:T(8,128)(2,1)S(1)}, bf16[4,32,32,512]{3,2,1,0:T(8,128)(2,1)}, u32[]{:S(2)}) copy-start(bf16[4,32,32,512]{3,2,1,0:T(8,128)(2,1)} %x_ref.1) | copy-start | bytes 12582916
